TPU v7x, 32 devices: a whole 2x2x4 slice. The times are simulated.
32 devices in a mesh: band: 8 (over z, x), coef: 4 (over y, core).
Axes of the slice: x: 2, y: 2, z: 4, core: 2. Of those that a mesh axis runs over, the one named last changes fastest.
Arguments:
- coeffs: float32 [1024, 262144], P('band', 'coef'), may hold values from -320 to 320
- ref_block: float32 [1024, 262144], P('band', 'coef'), may hold values from -0.01171875 to 0.01171875
- index_map: int32 [262144], P('coef'), may hold values from 0 to 65535, as said below
- band_group: int32 [1024], P('band'), may hold values from 0 to 15
Outputs:
- ortho: float32 [1024, 262144], P('band', 'coef')
- band_residual: float32 [1024], P('band')
- group_residual: float32 [16], replicated
Inputs may be any that keep to these rules, and one draw needn't show every extreme that they name: Within each aligned slab of 65536 coefficients, index_map holds every number of 0 to 65535 once.
All inputs are finite; a program needn't handle non-finite values.
Results may differ from a plain program's by a relative error of at most 0.000098.
Values sent between devices are 32-bit elements; how exact they have to be, the bound alone decides.
A program may use at most 384 MiB of HBM per device.

v0:
```python
import jax
import jax.numpy as jnp
from jax import lax
from jax.sharding import PartitionSpec as P

NGROUPS = 16
BLOCK = 128
ROWS = 256


def high(a, b):
    return jnp.dot(a, b, precision=lax.Precision.HIGH, preferred_element_type=jnp.float32)


def highest(a, b):
    return jnp.dot(a, b, precision=lax.Precision.HIGHEST, preferred_element_type=jnp.float32)


def inverse_factor(margin):
    size = margin.shape[0]
    eye = jnp.eye(BLOCK, dtype=jnp.float32)
    rest = margin
    below = jnp.zeros((size, 0), jnp.float32)
    rows = []
    for start in range(0, size, BLOCK):
        corner = lax.linalg.cholesky(rest[:BLOCK, :BLOCK], symmetrize_input=False)
        inv = lax.linalg.triangular_solve(corner, eye, left_side=True, lower=True)
        row = jnp.concatenate([highest(inv, below[:BLOCK]), inv], axis=1) if start else inv
        rows.append(jnp.pad(row, ((0, 0), (0, size - row.shape[1]))))
        if start + BLOCK < size:
            panel = highest(rest[BLOCK:, :BLOCK], inv.T)
            change = highest(panel, row)
            below = jnp.pad(below[BLOCK:], ((0, 0), (0, BLOCK))) - change
            rest = rest[BLOCK:, BLOCK:] - highest(panel, panel.T)
    return jnp.concatenate(rows, axis=0)


def local(coeffs, ref_block, index_map, band_group):
    devices = lax.axis_size("band")
    bands, slab = coeffs.shape
    part = slab // devices
    total = bands * devices
    pieces = coeffs.reshape(bands, devices, part).transpose(1, 0, 2)
    columns = lax.all_to_all(pieces, "band", split_axis=0, concat_axis=0, tiled=True)
    columns = columns.reshape(total, part)
    _, inverse = lax.sort((index_map, jnp.arange(slab, dtype=jnp.int32)), num_keys=1)
    ref_own = jnp.take(ref_block, inverse, axis=1, unique_indices=True, mode="clip")
    tops = range(0, total, ROWS)
    strips = [high(columns[t : t + ROWS], columns[: t + ROWS].T) for t in tops]
    strips = lax.psum(jnp.concatenate(strips, axis=1), ("band", "coef"))
    lower, at = ([], 0)
    for t in tops:
        width = t + ROWS
        lower.append(jnp.pad(strips[:, at : at + width], ((0, 0), (0, total - width))))
        at += width
    lower = jnp.concatenate(lower, axis=0)
    low = jnp.tril(lower)
    margin = low + jnp.tril(lower, -1).T
    inv = inverse_factor(margin)
    ortho_cols = jnp.concatenate(
        [high(inv[t : t + ROWS, : t + ROWS], columns[: t + ROWS]) for t in tops], axis=0
    )
    back = lax.all_to_all(
        ortho_cols.reshape(devices, bands, part), "band", split_axis=0, concat_axis=0, tiled=True
    )
    ortho = back.transpose(1, 0, 2).reshape(bands, slab)
    squares = jnp.sum((ortho - ref_own) ** 2, axis=1)
    band_residual = jnp.sqrt(lax.psum(squares, "coef") + 1e-06)
    onehot = (band_group[:, None] == jnp.arange(NGROUPS, dtype=jnp.int32)[None, :]).astype(
        jnp.float32
    )
    terms = highest(band_residual, onehot)
    group_residual = lax.psum(terms, "band") * (NGROUPS / total)
    return (ortho, band_residual, group_residual)


def solution(mesh):
    return jax.shard_map(
        local,
        mesh=mesh,
        in_specs=(P("band", "coef"), P("band", "coef"), P("coef"), P("band")),
        out_specs=(P("band", "coef"), P("band"), P()),
        check_vma=False,
    )
```

profile of v0, /device:TPU:0, one launch (start us, length us, event | category | flops | bytes accessed | tf_op | source)
XLA Modules:
  0.0 2275.0 jit_solution(11808679882351079061)
XLA Ops:
  7.2 33.4 %copy.37 = f32[128,65536]{0,1:T(8,128)} copy(f32[128,65536]{1,0:T(8,128)} %param.7) | data formatting | bytes 67108864 | tf_op args[0]
  40.6 735.1 %all_to_all.10 = f32[8,128,8192]{1,2,0:T(8,128)} all-to-all(f32[8,128,8192]{1,2,0:T(8,128)} %bitcast.125), channel_id=1, replica_groups=mesh['band'=8,'coef'=4] {'band'}, dimensions={0} | all-to-all | bytes 67108864 | tf_op jit(solution)/shard_map/all_to_all | solution.py:44
  775.7 23.5 %fusion.100 = (f32[2,128,8192]{1,2,0:T(8,128)}, f32[2,128,8192]{1,2,0:T(8,128)}, f32[2,128,8192]{1,2,0:T(8,128)}, f32[2,128,8192]{1,2,0:T(8,128)}) fusion(f32[8,128,8192]{1,2,0:T(8,128)} %all_to_all.10), kind=kLoop, calls=%fused_computation.177 | loop fusion | bytes 67108864 | tf_op jit(solution)/shard_map/slice | solution.py:49
  799.2 8.9 copy.41
  808.2 16.9 slice.228
  825.1 24.7 %copy.42 = f32[6,128,8192]{2,1,0:T(8,128)} copy(f32[6,128,8192]{1,2,0:T(8,128)} %slice.228) | data formatting | bytes 50331648 | tf_op jit(solution)/shard_map/slice | solution.py:49
  849.8 9.0 copy.39
  858.7 11.4 slice.226
  870.2 17.5 copy.40
  887.6 8.9 copy.43
  896.5 8.9 copy.38
  905.5 14.1 fusion.101
  919.5 22.3 fusion.103
  941.8 12.9 fusion.102
  954.8 31.1 %copy.44 = f32[8,128,8192]{2,1,0:T(8,128)} copy(f32[8,128,8192]{1,2,0:T(8,128)} %all_to_all.10) | data formatting | bytes 67108864 | tf_op jit(solution)/shard_map/all_to_all | solution.py:44
  985.9 19.7 fusion.104
  1005.5 1.7 pad_maximum_fusion.1
  1007.3 135.5 %all-reduce.17.cloned.1.call-done = f32[256,2560]{0,1:T(8,128)} async-done(((f32[256,2560]{0,1:T(8,128)}), f32[256,2560]{0,1:T(8,128)}) %all-reduce.17.cloned.1.call-update) | async-done | bytes 2621456 | tf_op jit(solution)/shard_map/psum | solution.py:50
  1142.8 1.2 slice.232
  1145.1 1.8 slice_select_fusion
  1146.8 2.8 fusion.3
  1149.7 5.3 copy.48
  1155.0 3.7 bitcast_add_fusion
  1158.7 1.9 copy-done
  1160.6 11.7 custom-call.20
  1173.7 9.8 custom-call.21
  1183.8 1.5 fusion.19
  1185.3 1.3 convolution_subtract_fusion.8
  1186.6 4.6 slice_subtract_fusion
  1191.2 11.9 custom-call.22
  1204.4 9.8 custom-call.23
  1214.6 1.1 fusion.76
  1217.2 2.0 slice_subtract_fusion.1
  1220.8 11.7 custom-call.24
  1233.8 10.0 custom-call.25
  1244.6 1.4 fusion.29
  1246.0 2.9 slice_subtract_fusion.2
  1250.5 11.7 custom-call.26
  1263.5 9.8 custom-call.27
  1274.5 1.4 convolution_subtract_fusion.1
  1277.7 11.7 custom-call.28
  1290.8 9.8 custom-call.29
  1302.4 11.9 custom-call.30
  1315.6 9.8 custom-call.31
  1327.6 1.3 convolution_subtract_fusion.9
  1329.0 11.7 custom-call.32
  1342.0 9.8 custom-call.33
  1354.2 10.7 fusion.38
  1365.8 11.7 custom-call.34
  1378.8 9.8 custom-call.35
  1389.8 13.1 fusion.17
  1402.9 18.0 fusion.12
  1420.9 23.5 %fusion.6 = f32[256,8192]{1,0:T(8,128)} fusion(f32[1024,8192]{1,0:T(8,128)} %bitcast.119, f32[128,896]{1,0:T(8,128)S(1)} %pad_maximum_fusion.2, f32[128,128]{1,0:T(8,128)S(1)} %copy.56, f32[128,896]{1,0:T(8,128)S(1)} %fusion.105), kind=kOutput, calls=%fused_computation.35 | convolution fusion | flops 12885950464 | bytes 42926080 | tf_op jit(solution)/shard_map/dot_general | solution.py:12
  1444.4 23.6 %pad_maximum_fusion = f32[1024,8192]{1,0:T(8,128)} fusion(f32[256,8192]{1,0:T(8,128)} %fusion.6, f32[256,8192]{1,0:T(8,128)} %fusion.12, f32[256,8192]{1,0:T(8,128)} %fusion.17, f32[256,8192]{1,0:T(8,128)} %fusion.38), kind=kLoop, calls=%fused_computation.1 | loop fusion | flops 25165824 | bytes 67108864 | tf_op jit(solution)/shard_map/concatenate | solution.py:60
  1468.0 7.3 all-to-all-start.1
  1475.3 33.4 %copy.58 = f32[128,65536]{0,1:T(8,128)} copy(f32[128,65536]{1,0:T(8,128)} %param.8) | data formatting | bytes 67108864 | tf_op args[1]
  1508.8 25.5 %sort.15 = (s32[65536]{0:T(1024)}, s32[65536]{0:T(1024)S(1)}) sort(s32[65536]{0:T(1024)S(1)} %copy-done.5, s32[65536]{0:T(1024)S(1)} %iota.166), dimensions={0}, to_apply=%region_3.6 | sort | flops 1048576 | bytes 1048576 | tf_op jit(solution)/shard_map/sort | solution.py:46
  1534.3 226.1 %gather_fusion = f32[65536,128]{1,0:T(8,128)} fusion(f32[128,65536]{0,1:T(8,128)} %copy.58, s32[65536]{0:T(1024)S(1)} %broadcast_clamp_fusion), kind=kCustom, calls=%fused_computation | custom fusion | bytes 67371008 | tf_op jit(solution)/shard_map/jit(_take)/gather | solution.py:47
  1760.4 31.1 %copy.59 = f32[128,8,8192]{2,0,1:T(8,128)} copy(f32[128,8,8192]{0,2,1:T(8,128)} %bitcast.128) | data formatting | bytes 67108864 | tf_op jit(solution)/shard_map/jit(_take)/gather | solution.py:47
  1791.5 405.6 %all-to-all-done.1 = f32[8,128,8192]{2,1,0:T(8,128)} async-done(((f32[8,128,8192]{2,1,0:T(8,128)}), f32[8,128,8192]{2,1,0:T(8,128)}, u32[]{:S(2)}, u32[]{:S(2)}) %all-to-all-start.1) | async-done | bytes 33554464 | tf_op jit(solution)/shard_map/all_to_all | solution.py:63
  2197.1 20.9 fusion.1
  2218.0 5.7 psum.22
  2223.8 20.4 psum.23
  2244.8 22.9 %copy.64 = f32[8,16,8,8192]{3,2,0,1:T(8,128)} copy(f32[8,16,8,8192]{3,2,1,0:T(8,128)} %bitcast.34) | data formatting | bytes 67108864 | tf_op jit(solution)/shard_map/reshape | solution.py:66
  (103 shorter events, 29.4 us)
Async XLA Ops:
  7.2 1135.6 %all-reduce.17.cloned.1.call-start = ((), (), s32[]{:S(2)}) async-start(), calls=%async_computation.2 | async-start | bytes 5242880 | tf_op jit(solution)/shard_map/psum | solution.py:50
  1005.5 139.5 %copy-start.6 = (pred[1024]{0:T(1024)(128)(4,1)S(1)}, pred[1024]{0:T(1024)(128)(4,1)}, u32[]{:S(2)}) copy-start(pred[1024]{0:T(1024)(128)(4,1)} %constant.30.clone.1) | copy-start | bytes 3076
  1158.7 1.9 copy-start
  1219.3 1.5 copy-start.1
  1302.4 23.7 %copy-start.2 = (f32[384,384]{1,0:T(8,128)}, f32[384,384]{1,0:T(8,128)S(1)}, u32[]{:S(2)}) copy-start(f32[384,384]{1,0:T(8,128)S(1)} %convolution_subtract_fusion.6) | copy-start | bytes 1769476
  1354.2 35.4 %copy-start.3 = (f32[128,512]{1,0:T(8,128)S(1)}, f32[128,512]{1,0:T(8,128)}, u32[]{:S(2)}) copy-start(f32[128,512]{1,0:T(8,128)} %pad_maximum_fusion.5) | copy-start | bytes 786436
  1354.2 35.6 %copy-start.4 = (f32[128,384]{1,0:T(8,128)S(1)}, f32[128,384]{1,0:T(8,128)}, u32[]{:S(2)}) copy-start(f32[128,384]{1,0:T(8,128)} %pad_maximum_fusion.6) | copy-start | bytes 589828
  1468.0 729.0 %all-to-all-start.1 = ((f32[8,128,8192]{2,1,0:T(8,128)}), f32[8,128,8192]{2,1,0:T(8,128)}, u32[]{:S(2)}, u32[]{:S(2)}) async-start(f32[8,128,8192]{2,1,0:T(8,128)} %bitcast.124), calls=%async_computation.1 | async-start | bytes 67108864 | tf_op jit(solution)/shard_map/all_to_all | solution.py:63
  1475.3 33.5 %copy-start.5 = (s32[65536]{0:T(1024)S(1)}, s32[65536]{0:T(1024)}, u32[]{:S(2)}) copy-start(s32[65536]{0:T(1024)} %param.9) | copy-start | bytes 786436
  1791.5 432.1 %copy-start.7 = (s32[128]{0:T(128)S(1)}, s32[128]{0:T(128)}, u32[]{:S(2)}) copy-start(s32[128]{0:T(128)} %param.10) | copy-start | bytes 1540
  2223.6 44.0 %copy-start.8 = (f32[128]{0:T(128)}, f32[128]{0:T(128)S(1)}, u32[]{:S(2)}) copy-start(f32[128]{0:T(128)S(1)} %add_sqrt_fusion) | copy-start | bytes 1540
Sparse Core Ops, SparseCore 0:
  1007.4 135.3 all-reduce.16
where the time goes:
time: 2290 us; the launch traced here: 2270 us
  blocking collectives  761 us (33%)
  waiting for transfers between devices  541 us (24%)
  local copies, waits for them, and re-layouts  519 us (23%)
  other arithmetic  266 us (12%)
  matrix products  165 us (7%)
    all_to_all x1, blocking collectives, local(): lax.all_to_all(pieces, 'band', split_axis=0, concat_axis=0, tiled=True)  735 us
    all_to_all x1, waiting for transfers between devices, local(): lax.all_to_all(ortho_cols.reshape(devices, bands, part), 'band', split_ax...  406 us
    gather x2, local copies, waits for them, and re-layouts, local(): jnp.take(ref_block, inverse, axis=1, unique_indices=True, mode='clip')  257 us
    psum x1, waiting for transfers between devices, local(): strips = lax.psum(jnp.concatenate(strips, axis=1), ('band', 'coef'))  135 us
    dot_general x8, matrix products, high(): jnp.dot(a, b, precision=lax.Precision.HIGH, preferred_element_type=jnp.fl...  134 us
    slice x9, local copies, waits for them, and re-layouts, local(): strips = [high(columns[t:t + ROWS], columns[:t + ROWS].T) for t in tops]  130 us
    another operation x24, other arithmetic, inverse_factor(): corner = lax.linalg.cholesky(rest[:BLOCK, :BLOCK], symmetrize_input=False)  99.4 us
    another operation x16, other arithmetic, inverse_factor(): inv = lax.linalg.triangular_solve(corner, eye, left_side=True, lower=True)  83.9 us
  transfers between devices with their start and end apart: 2, of which 2 were waited for; matrix products, arithmetic and copies ran while one was open for 14% of the time, Pallas kernels for 0%

commit v1 on v0

--- a/solution.py
+++ b/solution.py
@@ -47,7 +47,7 @@
     ref_own = jnp.take(ref_block, inverse, axis=1, unique_indices=True, mode="clip")
     tops = range(0, total, ROWS)
     strips = [high(columns[t : t + ROWS], columns[: t + ROWS].T) for t in tops]
-    strips = lax.psum(jnp.concatenate(strips, axis=1), ("band", "coef"))
+    strips = jnp.sum(lax.all_gather(jnp.concatenate(strips, axis=1), ("band", "coef")), axis=0)
     lower, at = ([], 0)
     for t in tops:
         width = t + ROWS

time: 2290 us -> 2630 us (1.15)
  waiting for transfers between devices: 541 us -> 842 us
  other arithmetic: 266 us -> 300 us
    all_gather x0 -> x1, waiting for transfers between devices: none -> 435 us  [local(): lax.all_gather(jnp.concatenate(strips, axis=1), ('band', 'coef'))]
    psum x1 -> x0, waiting for transfers between devices: 135 us -> none  [local(): strips = lax.psum(jnp.concatenate(strips, axis=1), ('band', 'coef'))]
    unnamed x20 -> x24, local copies, waits for them, and re-layouts: 68.8 us -> 75.5 us
  transfers between devices with their start and end apart: 2 -> 2, of which waited for: 2 -> 2; matrix products, arithmetic and copies ran while one was open for 14% -> 12% of each run, Pallas kernels for 0% -> 0%
where the time goes in v1:
time: 2630 us; the launch traced here: 2620 us
  waiting for transfers between devices  842 us (32%)
  blocking collectives  761 us (29%)
  local copies, waits for them, and re-layouts  527 us (20%)
  other arithmetic  300 us (11%)
  matrix products  162 us (6%)
    all_to_all x1, blocking collectives, local(): lax.all_to_all(pieces, 'band', split_axis=0, concat_axis=0, tiled=True)  735 us
    all_gather x1, waiting for transfers between devices, local(): lax.all_gather(jnp.concatenate(strips, axis=1), ('band', 'coef'))  435 us
    all_to_all x1, waiting for transfers between devices, local(): lax.all_to_all(ortho_cols.reshape(devices, bands, part), 'band', split_ax...  407 us
    gather x2, local copies, waits for them, and re-layouts, local(): jnp.take(ref_block, inverse, axis=1, unique_indices=True, mode='clip')  257 us
    dot_general x8, matrix products, high(): jnp.dot(a, b, precision=lax.Precision.HIGH, preferred_element_type=jnp.fl...  131 us
    slice x9, local copies, waits for them, and re-layouts, local(): strips = [high(columns[t:t + ROWS], columns[:t + ROWS].T) for t in tops]  130 us
    another operation x24, other arithmetic, inverse_factor(): corner = lax.linalg.cholesky(rest[:BLOCK, :BLOCK], symmetrize_input=False)  99.5 us
    another operation x16, other arithmetic, inverse_factor(): inv = lax.linalg.triangular_solve(corner, eye, left_side=True, lower=True)  84.1 us
  transfers between devices with their start and end apart: 2, of which 2 were waited for; matrix products, arithmetic and copies ran while one was open for 12% of the time, Pallas kernels for 0%

profile of v1, /device:TPU:0, one launch (start us, length us, event | category | flops | bytes accessed | tf_op | source)
XLA Modules:
  0.0 2615.4 jit_solution(13440119646837093365)
XLA Ops:
  7.2 33.4 %copy.54 = f32[128,65536]{0,1:T(8,128)} copy(f32[128,65536]{1,0:T(8,128)} %param.7) | data formatting | bytes 67108864 | tf_op args[0]
  40.6 735.1 %all_to_all.10 = f32[8,128,8192]{1,2,0:T(8,128)} all-to-all(f32[8,128,8192]{1,2,0:T(8,128)} %bitcast.126), channel_id=1, replica_groups=mesh['band'=8,'coef'=4] {'band'}, dimensions={0} | all-to-all | bytes 67108864 | tf_op jit(solution)/shard_map/all_to_all | solution.py:44
  775.7 23.5 fusion.100
  799.2 8.9 copy.58
  808.2 16.9 slice.228
  825.1 24.7 copy.59
  849.8 8.9 copy.56
  858.7 11.4 slice.226
  870.1 17.5 copy.57
  887.6 8.9 copy.60
  896.5 8.9 copy.55
  905.4 14.1 fusion.102
  919.5 17.2 fusion.104
  936.7 13.7 fusion.103
  950.4 31.1 %copy.61 = f32[8,128,8192]{2,1,0:T(8,128)} copy(f32[8,128,8192]{1,2,0:T(8,128)} %all_to_all.10) | data formatting | bytes 67108864 | tf_op jit(solution)/shard_map/all_to_all | solution.py:44
  981.5 21.1 fusion.105
  1002.6 1.8 pad_maximum_fusion.1
  1004.4 435.3 %all-gather.3.cloned.1.call-done = f32[8192,2560]{1,0:T(8,128)} async-done(((f32[256,2560]{1,0:T(8,128)}), f32[8192,2560]{1,0:T(8,128)}) %all-gather.3.cloned.1.call-update) | async-done | bytes 83886096 | tf_op jit(solution)/shard_map/all_gather | solution.py:50
  1439.7 26.0 reduce_sum.18
  1465.8 1.5 fusion.101
  1469.1 2.5 copy.81
  1471.7 1.6 copy.84
  1473.2 1.4 copy.83
  1475.9 1.4 broadcast_select_fusion
  1477.3 2.8 fusion.3
  1480.1 5.3 copy.67
  1485.5 12.0 bitcast_add_fusion
  1497.5 1.9 copy-done
  1499.4 11.7 custom-call.20
  1512.5 9.8 custom-call.21
  1522.6 1.5 fusion.19
  1525.4 4.6 slice_subtract_fusion
  1530.0 11.9 custom-call.22
  1543.3 9.8 custom-call.23
  1556.1 2.0 slice_subtract_fusion.1
  1559.6 11.7 custom-call.24
  1572.7 10.2 custom-call.25
  1583.6 1.4 fusion.29
  1585.0 2.9 slice_subtract_fusion.2
  1589.5 11.7 custom-call.26
  1602.6 9.8 custom-call.27
  1616.5 11.7 custom-call.28
  1629.6 9.8 custom-call.29
  1641.2 11.9 custom-call.30
  1654.5 9.8 custom-call.31
  1667.8 11.7 custom-call.32
  1680.9 9.8 custom-call.33
  1693.1 10.7 fusion.38
  1704.7 11.7 custom-call.34
  1717.8 9.8 custom-call.35
  1728.7 13.1 fusion.17
  1741.8 18.0 fusion.12
  1759.8 23.5 fusion.6
  1783.3 23.6 pad_maximum_fusion
  1806.9 7.3 all-to-all-start.1
  1814.2 33.4 %copy.77 = f32[128,65536]{0,1:T(8,128)} copy(f32[128,65536]{1,0:T(8,128)} %param.8) | data formatting | bytes 67108864 | tf_op args[1]
  1847.7 25.5 sort.15
  1873.2 226.1 %gather_fusion = f32[65536,128]{1,0:T(8,128)} fusion(f32[128,65536]{0,1:T(8,128)} %copy.77, s32[65536]{0:T(1024)S(1)} %broadcast_clamp_fusion), kind=kCustom, calls=%fused_computation | custom fusion | bytes 67371008 | tf_op jit(solution)/shard_map/jit(_take)/gather | solution.py:47
  2099.3 31.1 %copy.78 = f32[128,8,8192]{2,0,1:T(8,128)} copy(f32[128,8,8192]{0,2,1:T(8,128)} %bitcast.129) | data formatting | bytes 67108864 | tf_op jit(solution)/shard_map/jit(_take)/gather | solution.py:47
  2130.4 406.8 %all-to-all-done.1 = f32[8,128,8192]{2,1,0:T(8,128)} async-done(((f32[8,128,8192]{2,1,0:T(8,128)}), f32[8,128,8192]{2,1,0:T(8,128)}, u32[]{:S(2)}, u32[]{:S(2)}) %all-to-all-start.1) | async-done | bytes 33554464 | tf_op jit(solution)/shard_map/all_to_all | solution.py:63
  2537.2 20.9 fusion.1
  2558.1 6.1 psum.14
  2564.5 20.2 psum.15
  2585.2 22.9 copy.85
  (109 shorter events, 36.3 us)
Async XLA Ops:
  7.2 1432.6 %all-gather.3.cloned.1.call-start = ((), (), s32[]{:S(2)}) async-start(), calls=%async_computation.2 | async-start | bytes 86507520 | tf_op jit(solution)/shard_map/all_gather | solution.py:50
  1465.8 10.1 copy-start.6
  1497.5 1.9 copy-start
  1558.1 1.5 copy-start.1
  1641.2 23.8 copy-start.2
  1693.1 35.4 %copy-start.3 = (f32[128,512]{1,0:T(8,128)S(1)}, f32[128,512]{1,0:T(8,128)}, u32[]{:S(2)}) copy-start(f32[128,512]{1,0:T(8,128)} %pad_maximum_fusion.5) | copy-start | bytes 786436
  1693.1 35.6 %copy-start.4 = (f32[128,384]{1,0:T(8,128)S(1)}, f32[128,384]{1,0:T(8,128)}, u32[]{:S(2)}) copy-start(f32[128,384]{1,0:T(8,128)} %pad_maximum_fusion.6) | copy-start | bytes 589828
  1806.9 730.3 %all-to-all-start.1 = ((f32[8,128,8192]{2,1,0:T(8,128)}), f32[8,128,8192]{2,1,0:T(8,128)}, u32[]{:S(2)}, u32[]{:S(2)}) async-start(f32[8,128,8192]{2,1,0:T(8,128)} %bitcast.125), calls=%async_computation.1 | async-start | bytes 67108864 | tf_op jit(solution)/shard_map/all_to_all | solution.py:63
  1814.2 33.5 %copy-start.5 = (s32[65536]{0:T(1024)S(1)}, s32[65536]{0:T(1024)}, u32[]{:S(2)}) copy-start(s32[65536]{0:T(1024)} %param.9) | copy-start | bytes 786436
  2130.4 433.9 %copy-start.7 = (s32[128]{0:T(128)S(1)}, s32[128]{0:T(128)}, u32[]{:S(2)}) copy-start(s32[128]{0:T(128)} %param.10) | copy-start | bytes 1540
  2564.3 43.8 %copy-start.8 = (f32[128]{0:T(128)}, f32[128]{0:T(128)S(1)}, u32[]{:S(2)}) copy-start(f32[128]{0:T(128)S(1)} %add_sqrt_fusion) | copy-start | bytes 1540
Sparse Core Ops, SparseCore 0:
  1004.6 435.1 all-gather.2
